TPU v7x, 32 devices: a whole 2x2x4 slice. The times are simulated.
32 devices in a mesh: front: 4 (over y, core), row: 8 (over z, x).
Axes of the slice: x: 2, y: 2, z: 4, core: 2. Of those that a mesh axis runs over, the one named last changes fastest.
Arguments:
- rhs_diag: float32 [4, 32, 2048], P('front', None, 'row'), may hold values from -6 to 6
- rhs_off: float32 [4, 32, 12288], P('front', None, 'row'), may hold values from -6 to 6
- diag_factor: float32 [4, 2048, 2048], P('front', 'row'), may hold values from -0.125 to 0.125
- off_factor: float32 [4, 12288, 2048], P('front', 'row'), may hold values from -0.125 to 0.125
- diag_inverse: float32 [4, 4, 512, 512], P('front')
- pattern: int32 [4, 4, 96], P('front', None, 'row'), may hold values 0 or 1
- upd_vals: float32 [32, 4, 8, 4, 8, 128], P(None, 'front', 'row'), may hold values from -4 to 4
- upd_rows: int32 [4, 8, 4, 8, 128], P('front', 'row'), may hold values from 0 to 1791
Outputs:
- solved: float32 [4, 32, 2048], P('front', None, 'row')
- remainder: float32 [4, 32, 12288], P('front', None, 'row')
Inputs may be any that keep to these rules, and one draw needn't show every extreme that they name: `upd_rows`: relative rows of the receiving row block: below 256 a window row, else a row below the window; several entries may name one row.
All inputs are finite; a program needn't handle non-finite values. No bound on the sum of `pattern` on one device may be relied on, other than what follows from the above.
Results may differ from a plain program's by a relative error of at most 0.0001.
Values sent between devices are 32-bit elements; how exact they have to be, the bound alone decides.
A program may use at most 128 MiB of HBM per device.

v0:
```python
import jax
import jax.numpy as jnp
from jax import lax
from jax.sharding import PartitionSpec as P

W = 512
P_SIZE = 4
BR = 128


def local(rhs_diag, rhs_off, diag_factor, off_factor, diag_inverse, pattern, upd_vals, upd_rows):
    own_rows = diag_factor.shape[1]
    nrhs_count = upd_vals.shape[0]
    fronts_all = upd_vals.shape[3]
    groups_all = upd_vals.shape[4]
    slot_count = upd_vals.shape[5]
    flat_vals = upd_vals.reshape(nrhs_count, 1, fronts_all * groups_all, slot_count)
    arrived = lax.all_to_all(flat_vals, ("front", "row"), split_axis=2, concat_axis=1, tiled=True)
    received = arrived.reshape(nrhs_count, -1)
    targets = upd_rows.reshape(-1)
    combined = jnp.concatenate([rhs_diag[0], rhs_off[0]], axis=1)
    combined = combined.at[:, targets].add(received)
    upper = combined[:, :own_rows]
    lower = combined[:, own_rows:]
    diag_local = diag_factor[0]
    off_local = off_factor[0]
    inverse = diag_inverse[0]
    mask_rows = jnp.repeat(pattern[0].astype(jnp.float32), BR, axis=1)
    group = lax.axis_index("row")
    positions = group * own_rows + lax.iota(jnp.int32, own_rows)
    columns = lax.iota(jnp.int32, W)
    highest = lax.Precision.HIGHEST
    contract = (((1,), (1,)), ((), ()))
    pieces = []
    for panel in range(P_SIZE):
        picker = (
            (positions[:, None] // W == panel) & (positions[:, None] % W == columns[None, :])
        ).astype(jnp.float32)
        partial_rhs = jnp.dot(upper, picker, precision=highest, preferred_element_type=jnp.float32)
        panel_rhs = lax.psum(partial_rhs, "row")
        piece = lax.dot_general(
            panel_rhs,
            inverse[panel],
            contract,
            precision=highest,
            preferred_element_type=jnp.float32,
        )
        pieces.append(piece)
        upper = upper - lax.dot_general(
            piece,
            diag_local[:, panel * W : (panel + 1) * W],
            contract,
            precision=highest,
            preferred_element_type=jnp.float32,
        )
        term = lax.dot_general(
            piece,
            off_local[:, panel * W : (panel + 1) * W],
            contract,
            precision=highest,
            preferred_element_type=jnp.float32,
        )
        lower = lower - term * mask_rows[panel][None, :]
    solution = jnp.concatenate(pieces, axis=1)
    own_solution = lax.dynamic_slice_in_dim(solution, group * own_rows, own_rows, 1)
    return (own_solution[None], lower[None])


def solution(mesh):
    in_specs = (
        P("front", None, "row"),
        P("front", None, "row"),
        P("front", "row", None),
        P("front", "row", None),
        P("front", None, None, None),
        P("front", None, "row"),
        P(None, "front", "row", None, None, None),
        P("front", "row", None, None, None),
    )
    out_specs = (P("front", None, "row"), P("front", None, "row"))
    return jax.shard_map(local, mesh=mesh, in_specs=in_specs, out_specs=out_specs, check_vma=False)
```

profile of v0, /device:TPU:0, one launch (start us, length us, event | category | flops | bytes accessed | tf_op | source)
XLA Modules:
  0.0 367.9 jit_solution(12900171675111309321)
XLA Ops:
  7.2 2.1 copy.19
  9.3 7.3 %all-to-all-start = ((f32[32,1,32,128]{3,0,1,2:T(8,128)}), f32[32,1,32,128]{3,0,1,2:T(8,128)S(1)}, u32[]{:S(2)}, u32[]{:S(2)}) async-start(f32[32,1,32,128]{3,0,1,2:T(8,128)} %bitcast.4), calls=%async_computation | async-start | bytes 1048576 | tf_op jit(solution)/shard_map/all_to_all | solution.py:18
  16.6 0.0 all-reduce.5.cloned.1.call-start
  16.7 0.5 broadcast_compare_fusion.2
  17.2 0.7 convert_element_type.3
  17.9 0.9 pad_maximum_fusion
  18.9 0.7 broadcast_bitcast_fusion
  19.5 0.7 broadcast_bitcast_fusion.2
  20.2 0.5 broadcast_compare_fusion.4
  20.7 0.3 copy.21
  21.0 0.6 and_select_fusion
  21.6 0.7 compare_select_fusion
  22.3 10.5 %all-to-all-done = f32[32,1,32,128]{3,0,1,2:T(8,128)S(1)} async-done(((f32[32,1,32,128]{3,0,1,2:T(8,128)}), f32[32,1,32,128]{3,0,1,2:T(8,128)S(1)}, u32[]{:S(2)}, u32[]{:S(2)}) %all-to-all-start) | async-done | bytes 524320 | tf_op jit(solution)/shard_map/all_to_all | solution.py:18
  32.9 0.3 copy.20
  33.2 0.3 copy.29
  33.5 0.6 copy.22
  34.1 0.0 copy-start.4
  34.1 0.0 copy-start.7
  34.1 0.0 copy-start.6
  34.1 22.7 %scatter_fusion = f32[32,1792]{0,1:T(8,128)S(1)} fusion(f32[32,1792]{0,1:T(8,128)S(1)} %copy.21, s32[4096]{0:T(1024)S(1)} %bitcast.72, f32[4096,32]{1,0:T(8,128)S(1)} %copy.22), kind=kCustom, calls=%fused_computation | custom fusion | flops 131072 | bytes 1589248 | tf_op jit(solution)/shard_map/scatter-add | solution.py:22
  56.9 0.0 copy-done.4
  56.9 0.0 copy-done.7
  56.9 0.0 copy-start.5
  56.9 0.0 copy-start.3
  56.9 1.0 fusion.54
  57.9 0.0 all-reduce.5.cloned.1.call-update
  57.9 0.0 all-reduce.7.cloned.1.call-start
  58.0 0.1 copy.25
  58.1 67.0 %all-reduce.5.cloned.1.call-done = f32[32,512]{1,0:T(8,128)} async-done(((f32[32,512]{1,0:T(8,128)}), f32[32,512]{1,0:T(8,128)}) %all-reduce.5.cloned.1.call-update) | async-done | bytes 65552 | tf_op jit(solution)/shard_map/psum | solution.py:40
  125.1 2.3 fusion.41
  127.4 1.6 convolution_subtract_fusion.2
  129.0 0.0 copy-done.6
  129.0 1.0 fusion.56
  130.0 0.0 all-reduce.7.cloned.1.call-update
  130.1 0.0 all-reduce.9.cloned.1.call-start
  130.1 0.1 slice.100
  130.2 0.0 copy-start.2
  130.2 0.2 copy.26
  130.4 69.0 %all-reduce.7.cloned.1.call-done = f32[32,512]{1,0:T(8,128)} async-done(((f32[32,512]{1,0:T(8,128)}), f32[32,512]{1,0:T(8,128)}) %all-reduce.7.cloned.1.call-update) | async-done | bytes 65552 | tf_op jit(solution)/shard_map/psum | solution.py:40
  199.4 2.3 fusion.39
  201.7 1.6 convolution_subtract_fusion.1
  203.3 0.0 copy-done.5
  203.4 1.0 fusion.58
  204.4 0.0 all-reduce.9.cloned.1.call-update
  204.4 0.2 all-reduce.11.cloned.1.call-start
  204.6 0.0 copy-done.3
  204.6 4.8 %fusion.23 = f32[32,1536]{1,0:T(8,128)S(1)} fusion(f32[32,512]{1,0:T(8,128)S(1)} %fusion.39, f32[1536,2048]{1,0:T(8,128)} %bitcast.62, f32[1536]{0:T(1024)S(1)} %copy-done.3), kind=kOutput, calls=%fused_computation.14 | convolution fusion | flops 302039040 | bytes 3414016 | tf_op jit(solution)/shard_map/dot_general | solution.py:56
  209.4 0.0 copy-start.1
  209.4 64.3 %all-reduce.9.cloned.1.call-done = f32[32,512]{1,0:T(8,128)} async-done(((f32[32,512]{1,0:T(8,128)}), f32[32,512]{1,0:T(8,128)}) %all-reduce.9.cloned.1.call-update) | async-done | bytes 65552 | tf_op jit(solution)/shard_map/psum | solution.py:40
  273.7 2.3 fusion.37
  276.1 1.6 convolution_subtract_fusion
  277.7 1.0 fusion.60
  278.7 0.0 copy-start
  278.7 0.0 all-reduce.11.cloned.1.call-update
  278.7 0.0 copy-done.2
  278.7 4.8 %fusion.26 = f32[32,1536]{1,0:T(8,128)S(1)} fusion(f32[32,512]{1,0:T(8,128)S(1)} %fusion.37, f32[1536,2048]{1,0:T(8,128)} %bitcast.63, f32[1536]{0:T(1024)S(1)} %copy-done.2), kind=kOutput, calls=%fused_computation.15 | convolution fusion | flops 302039040 | bytes 3414016 | tf_op jit(solution)/shard_map/dot_general | solution.py:56
  283.5 64.5 %all-reduce.11.cloned.1.call-done = f32[32,512]{1,0:T(8,128)} async-done(((f32[32,512]{1,0:T(8,128)}), f32[32,512]{1,0:T(8,128)}) %all-reduce.11.cloned.1.call-update) | async-done | bytes 65552 | tf_op jit(solution)/shard_map/psum | solution.py:40
  348.1 2.3 fusion.35
  350.4 0.0 copy-done.1
  350.4 4.8 %fusion.29 = f32[32,1536]{1,0:T(8,128)S(1)} fusion(f32[32,512]{1,0:T(8,128)S(1)} %fusion.35, f32[1536,2048]{1,0:T(8,128)} %bitcast.64, f32[1536]{0:T(1024)S(1)} %copy-done.1), kind=kOutput, calls=%fused_computation.16 | convolution fusion | flops 302039040 | bytes 3414016 | tf_op jit(solution)/shard_map/dot_general | solution.py:56
  355.2 0.6 fusion.73
  355.8 0.0 copy-done
  355.8 5.5 %fusion.32 = f32[1,32,1536]{2,1,0:T(8,128)} fusion(f32[32,1536]{1,0:T(8,128)S(1)} %fusion.29, f32[32,1536]{1,0:T(8,128)S(1)} %fusion.26, f32[32,1536]{1,0:T(8,128)S(1)} %fusion.23, f32[32,1536]{1,0:T(8,128)S(1)} %copy.26, f32[32,512]{1,0:T(8,128)S(1)} %fusion.41, f32[1536,2048]{1,0:T(8,128)} %bitcast.65, f32[1536]{0:T(1024)S(1)} %copy-done), kind=kOutput, calls=%fused_computation.17 | convolution fusion | flops 302235648 | bytes 4200448 | tf_op jit(solution)/shard_map/dot_general | solution.py:56
  (4 shorter events, 0.0 us)
Async XLA Ops:
  9.3 23.6 %all-to-all-start = ((f32[32,1,32,128]{3,0,1,2:T(8,128)}), f32[32,1,32,128]{3,0,1,2:T(8,128)S(1)}, u32[]{:S(2)}, u32[]{:S(2)}) async-start(f32[32,1,32,128]{3,0,1,2:T(8,128)} %bitcast.4), calls=%async_computation | async-start | bytes 1048576 | tf_op jit(solution)/shard_map/all_to_all | solution.py:18
  16.6 108.5 %all-reduce.5.cloned.1.call-start = ((), (), s32[]{:S(2)}) async-start(), calls=%async_computation.1 | async-start | bytes 131072 | tf_op jit(solution)/shard_map/psum | solution.py:40
  34.1 22.8 %copy-start.4 = (s32[256]{0:T(256)S(1)}, s32[256]{0:T(256)}, u32[]{:S(2)}) copy-start(s32[256]{0:T(256)} %and_select_fusion) | copy-start | bytes 3076
  34.1 22.8 %copy-start.7 = (pred[256]{0:T(512)(128)(4,1)S(1)}, pred[256]{0:T(512)(128)(4,1)}, u32[]{:S(2)}) copy-start(pred[256]{0:T(512)(128)(4,1)} %broadcast_compare_fusion.2) | copy-start | bytes 772
  34.1 94.9 %copy-start.6 = (pred[256]{0:T(512)(128)(4,1)S(1)}, pred[256]{0:T(512)(128)(4,1)}, u32[]{:S(2)}) copy-start(pred[256]{0:T(512)(128)(4,1)} %broadcast_compare_fusion.4) | copy-start | bytes 772
  56.9 146.5 %copy-start.5 = (s32[256]{0:T(256)S(1)}, s32[256]{0:T(256)}, u32[]{:S(2)}) copy-start(s32[256]{0:T(256)} %and_select_fusion) | copy-start | bytes 3076
  56.9 147.7 %copy-start.3 = (f32[1536]{0:T(1024)S(1)}, f32[1536]{0:T(1024)}, u32[]{:S(2)}) copy-start(f32[1536]{0:T(1024)} %get-tuple-element.8) | copy-start | bytes 18436
  57.9 141.5 %all-reduce.7.cloned.1.call-start = ((), (), s32[]{:S(2)}) async-start(), calls=%async_computation.2 | async-start | bytes 131072 | tf_op jit(solution)/shard_map/psum | solution.py:40
  130.1 143.7 %all-reduce.9.cloned.1.call-start = ((), (), s32[]{:S(2)}) async-start(), calls=%async_computation.3 | async-start | bytes 131072 | tf_op jit(solution)/shard_map/psum | solution.py:40
  130.2 148.5 %copy-start.2 = (f32[1536]{0:T(1024)S(1)}, f32[1536]{0:T(1024)}, u32[]{:S(2)}) copy-start(f32[1536]{0:T(1024)} %get-tuple-element.7) | copy-start | bytes 18436
  204.4 143.7 %all-reduce.11.cloned.1.call-start = ((), (), s32[]{:S(2)}) async-start(), calls=%async_computation.4 | async-start | bytes 131072 | tf_op jit(solution)/shard_map/psum | solution.py:40
  209.4 140.9 %copy-start.1 = (f32[1536]{0:T(1024)S(1)}, f32[1536]{0:T(1024)}, u32[]{:S(2)}) copy-start(f32[1536]{0:T(1024)} %get-tuple-element.6) | copy-start | bytes 18436
  278.7 77.2 %copy-start = (f32[1536]{0:T(1024)S(1)}, f32[1536]{0:T(1024)}, u32[]{:S(2)}) copy-start(f32[1536]{0:T(1024)} %get-tuple-element.9) | copy-start | bytes 18436
Sparse Core Ops, SparseCore 0:
  58.0 66.9 all-reduce.4
  130.2 69.1 all-reduce.6
  204.5 69.1 all-reduce.8
  278.8 69.1 all-reduce.10
where the time goes:
time: 369 us; the launch traced here: 368 us
  waiting for transfers between devices  275 us (75%)
  matrix products  37.9 us (10%)
  other arithmetic  27.4 us (7%)
  between operations  14 us (4%)
  starting transfers between devices  7.67 us (2%)
  local copies, waits for them, and re-layouts  5.4 us (1%)
    psum x4, waiting for transfers between devices, local(): panel_rhs = lax.psum(partial_rhs, 'row')  265 us
    scatter-add x1, other arithmetic, local(): combined = combined.at[:, targets].add(received)  22.7 us
    dot_general x4, matrix products, local(): lax.dot_general(piece, off_local[:, panel * W:(panel + 1) * W], contract,...  19.9 us
    all_to_all x1, waiting for transfers between devices, local(): lax.all_to_all(flat_vals, ('front', 'row'), split_axis=2, concat_axis=1,...  10.5 us
    dot_general x4, matrix products, local(): lax.dot_general(panel_rhs, inverse[panel], contract, precision=highest, p...  9.18 us
  transfers between devices with their start and end apart: 5, of which 5 were waited for; matrix products, arithmetic and copies ran while one was open for 4% of the time, Pallas kernels for 0%

commit v1 on v0

--- a/solution.py
+++ b/solution.py
@@ -6,6 +6,11 @@
 W = 512
 P_SIZE = 4
 BR = 128
+
+
+def gather_and_add(array, axis):
+    parts = lax.all_gather(array, axis)
+    return jnp.sum(parts, axis=0)
 
 
 def local(rhs_diag, rhs_off, diag_factor, off_factor, diag_inverse, pattern, upd_vals, upd_rows):
@@ -37,7 +42,7 @@
             (positions[:, None] // W == panel) & (positions[:, None] % W == columns[None, :])
         ).astype(jnp.float32)
         partial_rhs = jnp.dot(upper, picker, precision=highest, preferred_element_type=jnp.float32)
-        panel_rhs = lax.psum(partial_rhs, "row")
+        panel_rhs = gather_and_add(partial_rhs, "row")
         piece = lax.dot_general(
             panel_rhs,
             inverse[panel],

time: 369 us -> 213 us (0.58)
  waiting for transfers between devices: 275 us -> 8.71 us
  blocking collectives: 0 us -> 125 us
  between operations: 14 us -> 0.92 us
    psum x4 -> x0, waiting for transfers between devices: 265 us -> none  [local(): panel_rhs = lax.psum(partial_rhs, 'row')]
    all_gather x0 -> x4, blocking collectives: none -> 125 us  [gather_and_add(): parts = lax.all_gather(array, axis)]
  transfers between devices with their start and end apart: 5 -> 1, of which waited for: 5 -> 1; matrix products, arithmetic and copies ran while one was open for 4% -> 4% of each run, Pallas kernels for 0% -> 0%
where the time goes in v1:
time: 213 us; the launch traced here: 212 us
  blocking collectives  125 us (59%)
  matrix products  35.3 us (17%)
  other arithmetic  28.7 us (13%)
  waiting for transfers between devices  8.71 us (4%)
  starting transfers between devices  7.33 us (3%)
  local copies, waits for them, and re-layouts  6.05 us (3%)
    all_gather x4, blocking collectives, gather_and_add(): parts = lax.all_gather(array, axis)  125 us
    scatter-add x1, other arithmetic, local(): combined = combined.at[:, targets].add(received)  22.7 us
    dot_general x4, matrix products, local(): lax.dot_general(piece, off_local[:, panel * W:(panel + 1) * W], contract,...  19.9 us
    dot_general x4, matrix products, local(): lax.dot_general(panel_rhs, inverse[panel], contract, precision=highest, p...  9.04 us
    all_to_all x1, waiting for transfers between devices, local(): lax.all_to_all(flat_vals, ('front', 'row'), split_axis=2, concat_axis=1,...  8.71 us
    all_to_all x1, starting transfers between devices, local(): lax.all_to_all(flat_vals, ('front', 'row'), split_axis=2, concat_axis=1,...  7.33 us
    dot_general x3, matrix products, local(): lax.dot_general(piece, diag_local[:, panel * W:(panel + 1) * W], contract...  4.84 us
  transfers between devices with their start and end apart: 1, of which 1 were waited for; matrix products, arithmetic and copies ran while one was open for 4% of the time, Pallas kernels for 0%

profile of v1, /device:TPU:0, one launch (start us, length us, event | category | flops | bytes accessed | tf_op | source)
XLA Modules:
  0.0 212.3 jit_solution(14548473937965722614)
XLA Ops:
  0.6 2.1 %copy.19 = f32[32,1,1,4,8,128]{5,0,4,3,2,1:T(8,128)} copy(f32[32,1,1,4,8,128]{5,4,3,2,1,0:T(8,128)} %param.14) | data formatting | bytes 1048576 | tf_op args[6]
  2.8 7.3 %all-to-all-start = ((f32[32,1,32,128]{3,0,1,2:T(8,128)}), f32[32,1,32,128]{3,0,1,2:T(8,128)S(1)}, u32[]{:S(2)}, u32[]{:S(2)}) async-start(f32[32,1,32,128]{3,0,1,2:T(8,128)} %bitcast.4), calls=%async_computation | async-start | bytes 1048576 | tf_op jit(solution)/shard_map/all_to_all | solution.py:23
  10.1 0.6 broadcast_compare_fusion.2
  10.7 0.5 broadcast_compare_fusion.4
  11.2 0.6 broadcast_compare_fusion.1
  11.8 0.7 convert_element_type.3
  12.5 0.7 broadcast_bitcast_fusion.2
  13.1 0.7 broadcast_bitcast_fusion.3
  13.8 0.9 pad_maximum_fusion
  14.7 0.7 broadcast_bitcast_fusion
  15.4 0.6 broadcast_compare_fusion
  16.0 0.3 copy.21
  16.3 0.6 and_select_fusion
  16.9 0.7 compare_select_fusion
  17.6 8.7 %all-to-all-done = f32[32,1,32,128]{3,0,1,2:T(8,128)S(1)} async-done(((f32[32,1,32,128]{3,0,1,2:T(8,128)}), f32[32,1,32,128]{3,0,1,2:T(8,128)S(1)}, u32[]{:S(2)}, u32[]{:S(2)}) %all-to-all-start) | async-done | bytes 524320 | tf_op jit(solution)/shard_map/all_to_all | solution.py:23
  26.3 0.3 copy.20
  26.6 0.3 copy.29
  27.0 0.6 copy.22
  27.6 0.0 copy-start.4
  27.6 0.0 copy-start.8
  27.6 22.7 %scatter_fusion = f32[32,1792]{0,1:T(8,128)S(1)} fusion(f32[32,1792]{0,1:T(8,128)S(1)} %copy.21, s32[4096]{0:T(1024)S(1)} %bitcast.80, f32[4096,32]{1,0:T(8,128)S(1)} %copy.22), kind=kCustom, calls=%fused_computation | custom fusion | flops 131072 | bytes 1589248 | tf_op jit(solution)/shard_map/scatter-add | solution.py:27
  50.3 0.0 copy-start.6
  50.3 0.0 copy-start.5
  50.3 0.1 slice.100
  50.4 0.0 copy-done.4
  50.4 0.0 copy-done.8
  50.4 0.4 fusion.54
  50.8 31.4 %all-gather = f32[256,512]{1,0:T(8,128)S(1)} all-gather(f32[32,512]{1,0:T(8,128)S(1)} %fusion.54), channel_id=2, replica_groups=mesh['front'=4,'row'=8] {'row'}, dimensions={0}, use_global_device_ids=true | all-gather | bytes 589824 | tf_op jit(solution)/shard_map/all_gather | solution.py:12
  82.2 0.1 copy.25
  82.3 0.0 copy-start.7
  82.3 2.3 %fusion.41 = f32[32,512]{1,0:T(8,128)S(1)} fusion(f32[32,512]{1,0:T(8,128)S(1)} %reduce_sum.36, f32[1,4,512,512]{3,2,1,0:T(8,128)} %param.12), kind=kOutput, calls=%fused_computation.27 | convolution fusion | flops 100663296 | bytes 1179648 | tf_op jit(solution)/shard_map/dot_general | solution.py:46
  84.6 1.6 convolution_subtract_fusion.2
  86.2 0.0 copy-done.6
  86.2 0.4 fusion.56
  86.6 31.3 %all-gather.1 = f32[256,512]{1,0:T(8,128)S(1)} all-gather(f32[32,512]{1,0:T(8,128)S(1)} %fusion.56), channel_id=3, replica_groups=mesh['front'=4,'row'=8] {'row'}, dimensions={0}, use_global_device_ids=true | all-gather | bytes 589824 | tf_op jit(solution)/shard_map/all_gather | solution.py:12
  117.9 0.0 copy-start.3
  117.9 2.3 %fusion.39 = f32[32,512]{1,0:T(8,128)S(1)} fusion(f32[32,512]{1,0:T(8,128)S(1)} %reduce_sum.37, f32[1,4,512,512]{3,2,1,0:T(8,128)} %param.12), kind=kOutput, calls=%fused_computation.25 | convolution fusion | flops 100663296 | bytes 1179648 | tf_op jit(solution)/shard_map/dot_general | solution.py:46
  120.2 1.6 convolution_subtract_fusion.1
  121.8 0.0 copy-done.5
  121.8 0.4 fusion.58
  122.2 31.3 %all-gather.2 = f32[256,512]{1,0:T(8,128)S(1)} all-gather(f32[32,512]{1,0:T(8,128)S(1)} %fusion.58), channel_id=4, replica_groups=mesh['front'=4,'row'=8] {'row'}, dimensions={0}, use_global_device_ids=true | all-gather | bytes 589824 | tf_op jit(solution)/shard_map/all_gather | solution.py:12
  153.5 0.0 copy-start.1
  153.5 2.3 %fusion.37 = f32[32,512]{1,0:T(8,128)S(1)} fusion(f32[32,512]{1,0:T(8,128)S(1)} %reduce_sum.38, f32[1,4,512,512]{3,2,1,0:T(8,128)} %param.12), kind=kOutput, calls=%fused_computation.23 | convolution fusion | flops 100663296 | bytes 1179648 | tf_op jit(solution)/shard_map/dot_general | solution.py:46
  155.8 1.6 convolution_subtract_fusion
  157.4 0.0 copy-done.7
  157.4 0.4 fusion.60
  157.8 31.4 %all-gather.3 = f32[256,512]{1,0:T(8,128)S(1)} all-gather(f32[32,512]{1,0:T(8,128)S(1)} %fusion.60), channel_id=5, replica_groups=mesh['front'=4,'row'=8] {'row'}, dimensions={0}, use_global_device_ids=true | all-gather | bytes 589824 | tf_op jit(solution)/shard_map/all_gather | solution.py:12
  189.2 2.3 %fusion.35 = f32[32,512]{1,0:T(8,128)S(1)} fusion(f32[32,512]{1,0:T(8,128)S(1)} %reduce_sum.39, f32[1,4,512,512]{3,2,1,0:T(8,128)} %param.12), kind=kOutput, calls=%fused_computation.21 | convolution fusion | flops 100663296 | bytes 1179648 | tf_op jit(solution)/shard_map/dot_general | solution.py:46
  191.5 0.0 copy-start.2
  191.5 0.0 copy-done.3
  191.5 4.8 %fusion.26 = f32[32,1536]{1,0:T(8,128)S(1)} fusion(f32[32,512]{1,0:T(8,128)S(1)} %fusion.37, f32[1536,2048]{1,0:T(8,128)} %bitcast.66, f32[1536]{0:T(1024)S(1)} %copy-done.3), kind=kOutput, calls=%fused_computation.15 | convolution fusion | flops 302039040 | bytes 3414016 | tf_op jit(solution)/shard_map/dot_general | solution.py:61
  196.3 0.0 copy-done.1
  196.3 0.0 copy-start
  196.3 4.8 %fusion.23 = f32[32,1536]{1,0:T(8,128)S(1)} fusion(f32[32,512]{1,0:T(8,128)S(1)} %fusion.39, f32[1536,2048]{1,0:T(8,128)} %bitcast.67, f32[1536]{0:T(1024)S(1)} %copy-done.1), kind=kOutput, calls=%fused_computation.14 | convolution fusion | flops 302039040 | bytes 3414016 | tf_op jit(solution)/shard_map/dot_general | solution.py:61
  201.1 0.2 copy.26
  201.4 0.0 copy-done.2
  201.4 4.8 %fusion.29 = f32[32,1536]{1,0:T(8,128)S(1)} fusion(f32[32,512]{1,0:T(8,128)S(1)} %fusion.35, f32[1536,2048]{1,0:T(8,128)} %bitcast.68, f32[1536]{0:T(1024)S(1)} %copy-done.2), kind=kOutput, calls=%fused_computation.16 | convolution fusion | flops 302039040 | bytes 3414016 | tf_op jit(solution)/shard_map/dot_general | solution.py:61
  206.2 0.6 fusion.73
  206.8 0.0 copy-done
  206.8 5.5 %fusion.32 = f32[1,32,1536]{2,1,0:T(8,128)} fusion(f32[32,1536]{1,0:T(8,128)S(1)} %fusion.29, f32[32,1536]{1,0:T(8,128)S(1)} %fusion.26, f32[32,1536]{1,0:T(8,128)S(1)} %fusion.23, f32[32,1536]{1,0:T(8,128)S(1)} %copy.26, f32[32,512]{1,0:T(8,128)S(1)} %fusion.41, f32[1536,2048]{1,0:T(8,128)} %bitcast.69, f32[1536]{0:T(1024)S(1)} %copy-done), kind=kOutput, calls=%fused_computation.17 | convolution fusion | flops 302235648 | bytes 4200448 | tf_op jit(solution)/shard_map/dot_general | solution.py:61
  (6 shorter events, 0.2 us)
Async XLA Ops:
  2.8 23.6 %all-to-all-start = ((f32[32,1,32,128]{3,0,1,2:T(8,128)}), f32[32,1,32,128]{3,0,1,2:T(8,128)S(1)}, u32[]{:S(2)}, u32[]{:S(2)}) async-start(f32[32,1,32,128]{3,0,1,2:T(8,128)} %bitcast.4), calls=%async_computation | async-start | bytes 1048576 | tf_op jit(solution)/shard_map/all_to_all | solution.py:23
  27.6 22.8 %copy-start.4 = (s32[256]{0:T(256)S(1)}, s32[256]{0:T(256)}, u32[]{:S(2)}) copy-start(s32[256]{0:T(256)} %and_select_fusion) | copy-start | bytes 3076
  27.6 22.8 %copy-start.8 = (pred[256]{0:T(512)(128)(4,1)S(1)}, pred[256]{0:T(512)(128)(4,1)}, u32[]{:S(2)}) copy-start(pred[256]{0:T(512)(128)(4,1)} %broadcast_compare_fusion.2) | copy-start | bytes 772
  50.3 35.9 %copy-start.6 = (pred[256]{0:T(512)(128)(4,1)S(1)}, pred[256]{0:T(512)(128)(4,1)}, u32[]{:S(2)}) copy-start(pred[256]{0:T(512)(128)(4,1)} %broadcast_compare_fusion.4) | copy-start | bytes 772
  50.3 71.5 %copy-start.5 = (pred[256]{0:T(512)(128)(4,1)S(1)}, pred[256]{0:T(512)(128)(4,1)}, u32[]{:S(2)}) copy-start(pred[256]{0:T(512)(128)(4,1)} %broadcast_compare_fusion.1) | copy-start | bytes 772
  82.3 75.1 %copy-start.7 = (pred[256]{0:T(512)(128)(4,1)S(1)}, pred[256]{0:T(512)(128)(4,1)}, u32[]{:S(2)}) copy-start(pred[256]{0:T(512)(128)(4,1)} %broadcast_compare_fusion) | copy-start | bytes 772
  117.9 73.6 %copy-start.3 = (f32[1536]{0:T(1024)S(1)}, f32[1536]{0:T(1024)}, u32[]{:S(2)}) copy-start(f32[1536]{0:T(1024)} %get-tuple-element.7) | copy-start | bytes 18436
  153.5 42.8 %copy-start.1 = (f32[1536]{0:T(1024)S(1)}, f32[1536]{0:T(1024)}, u32[]{:S(2)}) copy-start(f32[1536]{0:T(1024)} %broadcast_bitcast_fusion.2) | copy-start | bytes 18436
  191.5 9.9 %copy-start.2 = (f32[1536]{0:T(1024)S(1)}, f32[1536]{0:T(1024)}, u32[]{:S(2)}) copy-start(f32[1536]{0:T(1024)} %get-tuple-element.6) | copy-start | bytes 18436
  196.3 10.5 %copy-start = (f32[1536]{0:T(1024)S(1)}, f32[1536]{0:T(1024)}, u32[]{:S(2)}) copy-start(f32[1536]{0:T(1024)} %broadcast_bitcast_fusion.3) | copy-start | bytes 18436
